TPU v7x, 32 devices: a whole 2x2x4 slice. The times are simulated.
32 devices in a mesh: grp: 2 (over y), pos: 16 (over z, x, core).
Axes of the slice: x: 2, y: 2, z: 4, core: 2. Of those that a mesh axis runs over, the one named last changes fastest.
Arguments:
- object_field: float32 [2, 2048, 2048], P(None, 'grp', 'pos'), may hold values from -5 to 5
- probe_field: float32 [2, 256, 256], replicated, may hold values from -5 to 5
- patterns: float32 [96, 256, 256], P(('grp', 'pos')), may hold values from 0.05 to 5
- corners: int32 [2, 96], P(None, ('grp', 'pos')), may hold values from 0 to 1792, as said below
- counts: int32 [32], replicated, may hold values from 1 to 3, as said below
Outputs:
- object_new: float32 [2, 2048, 2048], P(None, 'grp', 'pos')
- probe_new: float32 [2, 256, 256], replicated
Inputs may be any that keep to these rules, and one draw needn't show every extreme that they name: `corners`: each slot's patch of 256 x 256 cells lies inside the object and inside its device's block of 1024 x 128 object cells extended by 128 cells on every side (the device at grp index a and pos index b holds rows a * 1024 to a * 1024 + 1023 and columns b * 128 to b * 128 + 127). The live slots of a device are its first counts[d] slots; some device has all 3 slots live.
All inputs are finite; a program needn't handle non-finite values.
Results may differ from a plain program's by a relative error of at most 0.00012.
Values sent between devices are 32-bit elements; how exact they have to be, the bound alone decides.
A program may use at most 64 MiB of HBM per device.

v0:
```python
import math
import jax
import jax.numpy as jnp
from jax import lax
from jax.sharding import PartitionSpec as P

M = 256
HALO = 128
step_object = 0.25
step_probe = 4.0


def padded(x, sides, width):
    for axis, dim in sides:
        peers, length = (lax.axis_size(axis), x.shape[dim])
        up = [(i, (i + 1) % peers) for i in range(peers - 1)]
        down = [(j, i) for i, j in up]
        last = lax.slice_in_dim(x, length - width, length, axis=dim)
        initial = lax.slice_in_dim(x, 0, width, axis=dim)
        before = lax.ppermute(last, axis, up)
        after = lax.ppermute(initial, axis, down)
        x = jnp.concatenate([before, x, after], axis=dim)
    return x


def product(left, right):
    return jnp.dot(left, right, precision=lax.Precision.HIGHEST, preferred_element_type=jnp.float32)


def left_mul(cos_part, sin_part, real_part, imag_part):
    return (
        product(cos_part, real_part) - product(sin_part, imag_part),
        product(cos_part, imag_part) + product(sin_part, real_part),
    )


def right_mul(real_part, imag_part, cos_part, sin_part):
    return (
        product(real_part, cos_part) - product(imag_part, sin_part),
        product(real_part, sin_part) + product(imag_part, cos_part),
    )


def dft_tables(order):
    indices = jnp.arange(order, dtype=jnp.int32)
    phases = indices[:, None] * indices[None, :] % order
    angles = phases.astype(jnp.float32) * (2.0 * math.pi / order)
    factor = 1.0 / math.sqrt(order)
    return (jnp.cos(angles) * factor, -jnp.sin(angles) * factor)


def far_field(wave, measured, cos_table, sin_table):
    front_re, front_im = left_mul(cos_table, sin_table, wave[0], wave[1])
    far_re, far_im = right_mul(front_re, front_im, cos_table, sin_table)
    excess = far_re * far_re + far_im * far_im - measured
    back_re, back_im = left_mul(cos_table, -sin_table, excess * far_re, excess * far_im)
    chi_re, chi_im = right_mul(back_re, back_im, cos_table, -sin_table)
    return jnp.stack((chi_re, chi_im))


def on_device(object_field, probe_field, patterns, corners, counts):
    tile_rows = object_field.shape[1]
    tile_cols = object_field.shape[2]
    slot_count = patterns.shape[0]
    pos_count = lax.axis_size("pos")
    grp_index = lax.axis_index("grp")
    pos_index = lax.axis_index("pos")
    device = grp_index * pos_count + pos_index
    own_count = counts[device]
    cos_table, sin_table = dft_tables(M)
    extended = padded(object_field, (("grp", 1), ("pos", 2)), HALO)
    row_local = corners[0] - grp_index * tile_rows + HALO
    col_local = corners[1] - pos_index * tile_cols + HALO

    def cut_patch(row_at, col_at):
        return lax.dynamic_slice(extended, (jnp.int32(0), row_at, col_at), (2, M, M))

    patches = jax.vmap(cut_patch)(row_local, col_local)
    waves = jnp.stack(
        (
            probe_field[0] * patches[:, 0] - probe_field[1] * patches[:, 1],
            probe_field[0] * patches[:, 1] + probe_field[1] * patches[:, 0],
        ),
        axis=1,
    )
    empty_results = jnp.zeros((slot_count, 2, M, M), jnp.float32)

    def solve_own(step, results):
        result = far_field(waves[step], patterns[step], cos_table, sin_table)
        return lax.dynamic_update_index_in_dim(results, result, step, 0)

    residuals = lax.fori_loop(0, own_count, solve_own, empty_results)

    def accumulate(step, totals):
        grad_ext, grad_probe = totals
        chi_re = residuals[step, 0]
        chi_im = residuals[step, 1]
        patch_re = patches[step, 0]
        patch_im = patches[step, 1]
        obj_part = jnp.stack(
            (
                probe_field[0] * chi_re + probe_field[1] * chi_im,
                probe_field[0] * chi_im - probe_field[1] * chi_re,
            )
        )
        prb_part = jnp.stack(
            (patch_re * chi_re + patch_im * chi_im, patch_re * chi_im - patch_im * chi_re)
        )
        anchor = (jnp.int32(0), row_local[step], col_local[step])
        current = lax.dynamic_slice(grad_ext, anchor, (2, M, M))
        grad_ext = lax.dynamic_update_slice(grad_ext, current + obj_part, anchor)
        return (grad_ext, grad_probe + prb_part)

    start_totals = (
        jnp.zeros(extended.shape, jnp.float32),
        jnp.zeros(probe_field.shape, jnp.float32),
    )
    grad_ext, grad_probe = lax.fori_loop(0, own_count, accumulate, start_totals)
    col_rims = jnp.concatenate((grad_ext[:, :, :HALO], grad_ext[:, :, -HALO:]), axis=2)
    col_arrived = padded(col_rims, (("pos", 2),), HALO)
    middle = grad_ext[:, :, HALO : HALO + tile_cols]
    middle = middle.at[:, :, :HALO].add(col_arrived[:, :, :HALO])
    middle = middle.at[:, :, tile_cols - HALO :].add(col_arrived[:, :, -HALO:])
    row_rims = jnp.concatenate((middle[:, :HALO], middle[:, -HALO:]), axis=1)
    row_arrived = padded(row_rims, (("grp", 1),), HALO)
    core = middle[:, HALO : HALO + tile_rows]
    core = core.at[:, :HALO].add(row_arrived[:, :HALO])
    core = core.at[:, tile_rows - HALO :].add(row_arrived[:, -HALO:])
    object_new = object_field - step_object * core
    live_total = jnp.sum(counts).astype(jnp.float32)
    share = lax.psum_scatter(grad_probe, "pos", scatter_dimension=1, tiled=True)
    share = lax.psum(share, "grp")
    row_share = M // pos_count
    mine = lax.dynamic_slice_in_dim(probe_field, pos_index * row_share, row_share, 1)
    new_rows = mine - step_probe * share / live_total
    probe_new = lax.all_gather(new_rows, "pos", axis=1, tiled=True)
    return (object_new, probe_new)


def solution(mesh):
    return jax.shard_map(
        on_device,
        mesh=mesh,
        in_specs=(
            P(None, "grp", "pos"),
            P(),
            P(("grp", "pos"), None, None),
            P(None, ("grp", "pos")),
            P(),
        ),
        out_specs=(P(None, "grp", "pos"), P()),
        check_vma=False,
    )
```

profile of v0, /device:TPU:0, one launch (start us, length us, event | category | flops | bytes accessed | tf_op | source)
XLA Modules:
  0.0 322.7 jit_solution(2919764576730867751)
XLA Ops:
  8.3 4.9 %collective-permute-start = (f32[2,128,128]{2,1,0:T(8,128)S(1)}, f32[2,128,128]{2,1,0:T(8,128)S(1)}, u32[]{:S(2)}, u32[]{:S(2)}) collective-permute-start(f32[2,128,128]{2,1,0:T(8,128)S(1)} %get-tuple-element.348), channel_id=1, source_target_pairs={{0,16},{1,17},{2,18},{3,19},{4,20},{5,21},{6,22},{7,23},{8,24},{9,... | collective-permute-start | bytes 393224 | tf_op jit(solution)/shard_map/ppermute | solution.py:20
  17.2 2.8 collective-permute-done.1
  24.4 3.7 %collective-permute-done.3 = f32[2,1280,128]{2,1,0:T(8,128)} collective-permute-done((f32[2,1280,128]{2,1,0:T(8,128)S(1)}, f32[2,1280,128]{2,1,0:T(8,128)}, u32[]{:S(2)}, u32[]{:S(2)}) %collective-permute-start.3) | collective-permute-done | bytes 1310752 | tf_op jit(solution)/shard_map/ppermute | solution.py:21
  28.2 3.4 %pad_maximum_fusion = f32[2,1280,384]{2,1,0:T(8,128)} fusion(f32[2,1280,128]{2,1,0:T(8,128)} %collective-permute-done.3, f32[2,1280,128]{2,1,0:T(8,128)S(1)} %constant_dynamic-update-slice_fusion, f32[2,1280,128]{2,1,0:T(8,128)S(1)} %collective-permute-done.2), kind=kLoop, calls=%fused_computation.139 | loop fusion | flops 1966080 | bytes 7864320 | tf_op jit(solution)/shard_map/concatenate | solution.py:22
  31.8 9.6 %while.33 = (s32[]{:T(128)}, f32[2,1280,384]{2,1,0:T(8,128)}, s32[3,3]{1,0:T(4,128)S(1)}, f32[3,2,256,256]{3,2,1,0:T(8,128)S(1)}, s32[]{:T(128)}) while((s32[]{:T(128)}, f32[2,1280,384]{2,1,0:T(8,128)}, s32[3,3]{1,0:T(4,128)S(1)}, f32[3,2,256,256]{3,2,1,0:T(8,128)S(1)}, s32[]{:T(128)}) %tuple.101), condition=%wide.while_cond.4, body=%wide.while_body.4.sunk | while | flops 2 | bytes 1048693 | solution.py:76
  32.4 2.5 bitcast_dynamic-update-slice_fusion.2
  35.7 2.5 bitcast_dynamic-update-slice_fusion.2
  38.9 2.5 bitcast_dynamic-update-slice_fusion.2
  44.2 30.9 %while.34 = (s32[]{:T(128)}, f32[3,2,256,256]{3,2,1,0:T(8,128)}, s32[]{:T(128)}, f32[3,2,256,256]{3,2,1,0:T(8,128)}, f32[3,256,256]{2,1,0:T(8,128)}, /*index=5*/s32[]{:T(128)}, s32[]{:T(128)}, s32[]{:T(128)}, s32[]{}) while((s32[]{:T(128)}, f32[3,2,256,256]{3,2,1,0:T(8,128)}, s32[]{:T(128)}, ...), condition=%wide.region_1.2_spmd.clone.clone, body=%wide.region_0.1_spmd.clone.clone.sunk | while | flops 3238789120 | bytes 12320939 | solution.py:92
  44.9 2.4 fusion.179
  47.3 2.4 convolution_subtract_fusion.7
  51.2 2.4 fusion.181
  53.7 2.4 convolution_add_fusion.6
  59.1 2.4 fusion.183
  75.1 2.1 broadcast_in_dim.18
  77.3 14.2 %while.32 = (s32[]{:T(128)}, f32[2,1280,384]{2,1,0:T(8,128)}, f32[2,256,256]{2,1,0:T(8,128)S(1)}, s32[]{:T(128)}, s32[3]{0:T(128)S(1)}, /*index=5*/s32[3]{0:T(12...) while((s32[]{:T(128)}, f32[2,1280,384]{2,1,0:T(8,128)}, ...), condition=%wide.region_3.4_spmd, body=%wide.region_2.3_spmd.sunk | while | flops 1310731 | bytes 6816019 | solution.py:118
  85.6 5.2 %dynamic_update_slice.13 = f32[2,1280,384]{2,1,0:T(8,128)} dynamic-update-slice(f32[2,1280,384]{2,1,0:T(8,128)} %get-tuple-element.545, f32[2,256,256]{2,1,0:T(8,128)S(1)} %get-tuple-element.473, s32[]{:T(128)} %constant.180.clone.1..sunk, s32[]{:T(128)S(6)} %select_n.163, s32[]{:T(128)S(6)} %select_n.164) | dynamic-update-slice | bytes 1048580 | tf_op jit(solution)/shard_map/while/body/dynamic_update_slice | solution.py:111
  91.5 3.2 fusion.116
  94.7 27.6 %collective-permute-start.4 = (f32[2,1280,128]{2,1,0:T(8,128)}, f32[2,1280,128]{2,1,0:T(8,128)S(1)}, u32[]{:S(2)}, u32[]{:S(2)}) collective-permute-start(f32[2,1280,128]{2,1,0:T(8,128)} %get-tuple-element.341), channel_id=1, source_target_pairs={{0,1},{1,2},{2,3},{3,4},{4,5},{5,6},{6,7},{7,8},{8,9},{9,10},{10,1... | collective-permute-start | bytes 3932168 | tf_op jit(solution)/shard_map/ppermute | solution.py:20
  124.9 147.0 %reduce-scatter.2.cloned.1.call-done = f32[2,16,256]{2,1,0:T(8,128)} async-done(((f32[2,256,256]{2,1,0:T(8,128)}), f32[2,16,256]{2,1,0:T(8,128)}) %reduce-scatter.2.cloned.1.call-update) | async-done | bytes 32784 | tf_op jit(solution)/shard_map/reduce_scatter | solution.py:131
  271.9 9.0 %psum.7 = f32[2,16,256]{2,1,0:T(8,128)S(1)} all-reduce(f32[2,16,256]{2,1,0:T(8,128)} %reduce-scatter.2.cloned.1.call-done), channel_id=1, replica_groups=mesh['grp'=2,'pos'=16] {'grp'}, use_global_device_ids=true, to_apply=%region_5.6 | all-reduce | flops 8192 | bytes 65536 | tf_op jit(solution)/shard_map/psum | solution.py:132
  282.8 2.5 collective-permute-start.6
  285.3 20.9 %all_gather.3 = f32[2,256,256]{2,1,0:T(8,128)S(1)} all-gather(f32[2,16,256]{2,1,0:T(8,128)S(1)} %divide_subtract_fusion), channel_id=1, replica_groups=mesh['grp'=2,'pos'=16] {'pos'}, dimensions={1}, use_global_device_ids=true | all-gather | bytes 557056 | tf_op jit(solution)/shard_map/all_gather | solution.py:136
  307.7 6.3 %collective-permute-done.7 = f32[2,128,128]{2,1,0:T(8,128)S(1)} collective-permute-done((f32[2,128,128]{2,1,0:T(8,128)S(1)}, f32[2,128,128]{2,1,0:T(8,128)S(1)}, u32[]{:S(2)}, u32[]{:S(2)}) %collective-permute-start.7) | collective-permute-done | bytes 131104 | tf_op jit(solution)/shard_map/ppermute | solution.py:21
  (73 shorter events, 42.4 us)
Async XLA Ops:
  7.2 15.6 %copy-start.5 = (s32[2,3]{1,0:T(2,128)S(1)}, s32[2,3]{1,0:T(2,128)}, u32[]{:S(2)}) copy-start(s32[2,3]{1,0:T(2,128)} %param.24) | copy-start | bytes 76
  7.2 15.7 %copy-start.6 = (s32[32]{0:T(128)S(1)}, s32[32]{0:T(128)}, u32[]{:S(2)}) copy-start(s32[32]{0:T(128)} %param.25) | copy-start | bytes 388
  7.2 16.4 %copy-start.1 = (f32[2,256,256]{2,1,0:T(8,128)S(1)}, f32[2,256,256]{2,1,0:T(8,128)}, u32[]{:S(2)}) copy-start(f32[2,256,256]{2,1,0:T(8,128)} %param.22) | copy-start | bytes 1572868
  7.2 264.7 %reduce-scatter.2.cloned.1.call-start = ((), (), s32[]{:S(2)}) async-start(), calls=%async_computation.1 | async-start | bytes 557056 | tf_op jit(solution)/shard_map/reduce_scatter | solution.py:131
  8.3 7.6 %collective-permute-start = (f32[2,128,128]{2,1,0:T(8,128)S(1)}, f32[2,128,128]{2,1,0:T(8,128)S(1)}, u32[]{:S(2)}, u32[]{:S(2)}) collective-permute-start(f32[2,128,128]{2,1,0:T(8,128)S(1)} %get-tuple-element.348), channel_id=1, source_target_pairs={{0,16},{1,17},{2,18},{3,19},{4,20},{5,21},{6,22},{7,23},{8,24},{9,... | collective-permute-start | bytes 393224 | tf_op jit(solution)/shard_map/ppermute | solution.py:20
  13.2 6.9 %collective-permute-start.1 = (f32[2,128,128]{2,1,0:T(8,128)S(1)}, f32[2,128,128]{2,1,0:T(8,128)S(1)}, u32[]{:S(2)}, u32[]{:S(2)}) collective-permute-start(f32[2,128,128]{2,1,0:T(8,128)S(1)} %get-tuple-element.347), channel_id=1, source_target_pairs={{16,0},{17,1},{18,2},{19,3},{20,4},{21,5},{22,6},{23,7},{24,8},{25... | collective-permute-start | bytes 393224 | tf_op jit(solution)/shard_map/ppermute | solution.py:21
  20.1 4.3 %collective-permute-start.2 = (f32[2,1280,128]{2,1,0:T(8,128)S(1)}, f32[2,1280,128]{2,1,0:T(8,128)S(1)}, u32[]{:S(2)}, u32[]{:S(2)}) collective-permute-start(f32[2,1280,128]{2,1,0:T(8,128)S(1)} %constant_dynamic-update-slice_fusion), channel_id=1, source_target_pairs={{0,1},{1,2},{2,3},{3,4},{4,5},{5,6},{6,7},{7,8},{8,9},{9,10},{10,1... | collective-permute-start | bytes 3932168 | tf_op jit(solution)/shard_map/ppermute | solution.py:20
  21.5 6.7 %collective-permute-start.3 = (f32[2,1280,128]{2,1,0:T(8,128)S(1)}, f32[2,1280,128]{2,1,0:T(8,128)}, u32[]{:S(2)}, u32[]{:S(2)}) collective-permute-start(f32[2,1280,128]{2,1,0:T(8,128)S(1)} %constant_dynamic-update-slice_fusion), channel_id=1, source_target_pairs={{1,0},{2,1},{3,2},{4,3},{5,4},{6,5},{7,6},{8,7},{9,8},{10,9},{11,1... | collective-permute-start | bytes 3932168 | tf_op jit(solution)/shard_map/ppermute | solution.py:21
  31.7 9.7 %copy-start.3 = (f32[256,256]{1,0:T(8,128)S(1)}, f32[256,256]{1,0:T(8,128)}, u32[]{:S(2)}) copy-start(f32[256,256]{1,0:T(8,128)} %get-tuple-element.349) | copy-start | bytes 786436
  31.7 9.7 %copy-start.4 = (f32[256,256]{1,0:T(8,128)S(1)}, f32[256,256]{1,0:T(8,128)}, u32[]{:S(2)}) copy-start(f32[256,256]{1,0:T(8,128)} %get-tuple-element.350) | copy-start | bytes 786436
  91.5 3.2 copy-start
  94.7 186.2 %collective-permute-start.4 = (f32[2,1280,128]{2,1,0:T(8,128)}, f32[2,1280,128]{2,1,0:T(8,128)S(1)}, u32[]{:S(2)}, u32[]{:S(2)}) collective-permute-start(f32[2,1280,128]{2,1,0:T(8,128)} %get-tuple-element.341), channel_id=1, source_target_pairs={{0,1},{1,2},{2,3},{3,4},{4,5},{5,6},{6,7},{7,8},{8,9},{9,10},{10,1... | collective-permute-start | bytes 3932168 | tf_op jit(solution)/shard_map/ppermute | solution.py:20
  122.3 158.6 %collective-permute-start.5 = (f32[2,1280,128]{2,1,0:T(8,128)S(1)}, f32[2,1280,128]{2,1,0:T(8,128)}, u32[]{:S(2)}, u32[]{:S(2)}) collective-permute-start(f32[2,1280,128]{2,1,0:T(8,128)S(1)} %get-tuple-element.342), channel_id=1, source_target_pairs={{1,0},{2,1},{3,2},{4,3},{5,4},{6,5},{7,6},{8,7},{9,8},{10,9},{11,1... | collective-permute-start | bytes 3932168 | tf_op jit(solution)/shard_map/ppermute | solution.py:21
  282.8 24.8 %collective-permute-start.6 = (f32[2,128,128]{2,1,0:T(8,128)S(1)}, f32[2,128,128]{2,1,0:T(8,128)S(1)}, u32[]{:S(2)}, u32[]{:S(2)}) collective-permute-start(f32[2,128,128]{2,1,0:T(8,128)S(1)} %get-tuple-element.346), channel_id=1, source_target_pairs={{0,16},{1,17},{2,18},{3,19},{4,20},{5,21},{6,22},{7,23},{8,24},{9,... | collective-permute-start | bytes 393224 | tf_op jit(solution)/shard_map/ppermute | solution.py:20
  306.1 7.9 %copy-start.2 = (f32[2,1024,128]{2,1,0:T(8,128)S(1)}, f32[2,1024,128]{2,1,0:T(8,128)}, u32[]{:S(2)}) copy-start(f32[2,1024,128]{2,1,0:T(8,128)} %param.21) | copy-start | bytes 3145732
  306.2 7.8 %collective-permute-start.7 = (f32[2,128,128]{2,1,0:T(8,128)S(1)}, f32[2,128,128]{2,1,0:T(8,128)S(1)}, u32[]{:S(2)}, u32[]{:S(2)}) collective-permute-start(f32[2,128,128]{2,1,0:T(8,128)S(1)} %get-tuple-element.345), channel_id=1, source_target_pairs={{16,0},{17,1},{18,2},{19,3},{20,4},{21,5},{22,6},{23,7},{24,8},{25... | collective-permute-start | bytes 393224 | tf_op jit(solution)/shard_map/ppermute | solution.py:21
Sparse Core Ops, SparseCore 0:
  123.8 148.0 reduce-scatter.1
where the time goes:
time: 325 us; the launch traced here: 323 us
  waiting for transfers between devices  161 us (50%)
  starting transfers between devices  41.7 us (13%)
  blocking collectives  29.8 us (9%)
  matrix products  28.4 us (9%)
  local copies, waits for them, and re-layouts  27.6 us (8%)
  between operations  15 us (5%)
  other arithmetic  11.9 us (4%)
  loops' own time  7.08 us (2%)
    reduce_scatter x1, waiting for transfers between devices, on_device(): share = lax.psum_scatter(grad_probe, 'pos', scatter_dimension=1, tiled=True)  147 us
    ppermute x4, starting transfers between devices, padded(): before = lax.ppermute(last, axis, up)  36.3 us
    dot_general x16, matrix products, product(): jnp.dot(left, right, precision=lax.Precision.HIGHEST, preferred_element_t...  28.4 us
    all_gather x1, blocking collectives, on_device(): probe_new = lax.all_gather(new_rows, 'pos', axis=1, tiled=True)  20.9 us
    ppermute x4, waiting for transfers between devices, padded(): after = lax.ppermute(initial, axis, down)  12.9 us
    gather x9, local copies, waits for them, and re-layouts  9.58 us
    psum x1, blocking collectives, on_device(): share = lax.psum(share, 'grp')  8.97 us
  transfers between devices with their start and end apart: 9, of which 5 were waited for; matrix products, arithmetic and copies ran while one was open for 1% of the time, Pallas kernels for 0%

commit v1 on v0

--- a/solution.py
+++ b/solution.py
@@ -8,6 +8,24 @@
 HALO = 128
 step_object = 0.25
 step_probe = 4.0
+
+
+def run_edges(block_here, bus_axis, array_axis):
+    n_blocks = jax.lax.axis_size(bus_axis)
+    stack_in = [(at, (at + 1) % n_blocks) for at in range(n_blocks)]
+
+    def report_the_outputs(lower):
+        if len(lower) == n_blocks:
+            return lower
+        s_next = report_the_outputs([jax.lax.ppermute(lower[0], bus_axis, stack_in), *lower])
+        return s_next
+
+    met_up = jnp.roll(
+        jnp.concatenate(report_the_outputs([block_here]), axis=array_axis),
+        (jax.lax.axis_index(bus_axis) + 1) * block_here.shape[array_axis],
+        axis=array_axis,
+    )
+    return met_up
 
 
 def padded(x, sides, width):
@@ -133,7 +151,7 @@
     row_share = M // pos_count
     mine = lax.dynamic_slice_in_dim(probe_field, pos_index * row_share, row_share, 1)
     new_rows = mine - step_probe * share / live_total
-    probe_new = lax.all_gather(new_rows, "pos", axis=1, tiled=True)
+    probe_new = run_edges(new_rows, "pos", array_axis=1)
     return (object_new, probe_new)
 
 

time: 325 us -> 402 us (1.24)
  the two profiles are of different devices: /device:TPU:0 before, /device:TPU:2 now
where the time goes in v1:
time: 402 us; the launch traced here: 400 us
  waiting for transfers between devices  276 us (69%)
  local copies, waits for them, and re-layouts  28.8 us (7%)
  matrix products  28.3 us (7%)
  starting transfers between devices  24.1 us (6%)
  between operations  15.2 us (4%)
  other arithmetic  11.8 us (3%)
  blocking collectives  8.91 us (2%)
  loops' own time  7.07 us (2%)
    reduce_scatter x1, waiting for transfers between devices, on_device(): share = lax.psum_scatter(grad_probe, 'pos', scatter_dimension=1, tiled=True)  144 us
    ppermute x15, waiting for transfers between devices, report_the_outputs(): jax.lax.ppermute(lower[0], bus_axis, stack_in)  83.1 us
    ppermute x4, waiting for transfers between devices, padded(): before = lax.ppermute(last, axis, up)  41 us
    dot_general x16, matrix products, product(): jnp.dot(left, right, precision=lax.Precision.HIGHEST, preferred_element_t...  28.3 us
    ppermute x4, starting transfers between devices, padded(): after = lax.ppermute(initial, axis, down)  12.7 us
    gather x9, local copies, waits for them, and re-layouts  9.85 us
    ppermute x4, starting transfers between devices, padded(): before = lax.ppermute(last, axis, up)  9.73 us
    psum x1, blocking collectives, on_device(): share = lax.psum(share, 'grp')  8.91 us
  transfers between devices with their start and end apart: 24, of which 22 were waited for; matrix products, arithmetic and copies ran while one was open for 2% of the time, Pallas kernels for 0%

profile of v1, /device:TPU:2, one launch (start us, length us, event | category | flops | bytes accessed | tf_op | source)
XLA Modules:
  0.0 400.3 jit_solution(13909269058838925098)
XLA Ops:
  20.5 3.6 collective-permute-start.3
  25.8 25.8 %collective-permute-done.2 = f32[2,1280,128]{2,1,0:T(8,128)S(1)} collective-permute-done((f32[2,1280,128]{2,1,0:T(8,128)S(1)}, f32[2,1280,128]{2,1,0:T(8,128)S(1)}, u32[]{:S(2)}, u32[]{:S(2)}) %collective-permute-start.2) | collective-permute-done | bytes 1310752 | tf_op jit(solution)/shard_map/ppermute | solution.py:38
  51.6 3.4 pad_maximum_fusion
  55.2 9.9 %while.33 = (s32[]{:T(128)}, f32[2,1280,384]{2,1,0:T(8,128)}, s32[3,3]{1,0:T(4,128)S(1)}, f32[3,2,256,256]{3,2,1,0:T(8,128)S(1)}, s32[]{:T(128)}) while((s32[]{:T(128)}, f32[2,1280,384]{2,1,0:T(8,128)}, s32[3,3]{1,0:T(4,128)S(1)}, f32[3,2,256,256]{3,2,1,0:T(8,128)S(1)}, s32[]{:T(128)}) %tuple.101), condition=%wide.while_cond.4, body=%wide.while_body.4.sunk | while | flops 2 | bytes 1048693 | solution.py:94
  67.9 30.8 %while.34 = (s32[]{:T(128)}, f32[3,2,256,256]{3,2,1,0:T(8,128)}, s32[]{:T(128)}, f32[3,2,256,256]{3,2,1,0:T(8,128)}, f32[3,256,256]{2,1,0:T(8,128)}, /*index=5*/s32[]{:T(128)}, s32[]{:T(128)}, s32[]{:T(128)}, s32[]{}) while((s32[]{:T(128)}, f32[3,2,256,256]{3,2,1,0:T(8,128)}, s32[]{:T(128)}, ...), condition=%wide.region_1.2_spmd.clone.clone, body=%wide.region_0.1_spmd.clone.clone.sunk | while | flops 3238789120 | bytes 12320939 | solution.py:110
  100.9 15.7 %while.32 = (s32[]{:T(128)}, f32[2,1280,384]{2,1,0:T(8,128)}, f32[2,256,256]{2,1,0:T(8,128)S(1)}, s32[]{:T(128)}, s32[3]{0:T(128)S(1)}, /*index=5*/s32[3]{0:T(12...) while((s32[]{:T(128)}, f32[2,1280,384]{2,1,0:T(8,128)}, ...), condition=%wide.region_3.4_spmd, body=%wide.region_2.3_spmd.sunk | while | flops 1310731 | bytes 6816019 | solution.py:136
  109.3 6.5 %dynamic_update_slice.13 = f32[2,1280,384]{2,1,0:T(8,128)} dynamic-update-slice(f32[2,1280,384]{2,1,0:T(8,128)} %get-tuple-element.545, f32[2,256,256]{2,1,0:T(8,128)S(1)} %get-tuple-element.473, s32[]{:T(128)} %constant.196.clone.1..sunk, s32[]{:T(128)S(6)} %select_n.177, s32[]{:T(128)S(6)} %select_n.178) | dynamic-update-slice | bytes 1048580 | tf_op jit(solution)/shard_map/while/body/dynamic_update_slice | solution.py:129
  118.7 143.7 %reduce-scatter.2.cloned.1.call-done = f32[2,16,256]{2,1,0:T(8,128)} async-done(((f32[2,256,256]{2,1,0:T(8,128)}), f32[2,16,256]{2,1,0:T(8,128)}) %reduce-scatter.2.cloned.1.call-update) | async-done | bytes 32784 | tf_op jit(solution)/shard_map/reduce_scatter | solution.py:149
  262.4 8.9 %psum.7 = f32[2,16,256]{2,1,0:T(8,128)S(1)} all-reduce(f32[2,16,256]{2,1,0:T(8,128)} %reduce-scatter.2.cloned.1.call-done), channel_id=1, replica_groups=mesh['grp'=2,'pos'=16] {'grp'}, use_global_device_ids=true, to_apply=%region_5.6 | all-reduce | flops 8192 | bytes 65536 | tf_op jit(solution)/shard_map/psum | solution.py:150
  282.5 4.0 collective-permute-done.11
  286.7 5.8 %collective-permute-done.12 = f32[2,16,256]{2,1,0:T(8,128)S(1)} collective-permute-done((f32[2,16,256]{2,1,0:T(8,128)S(1)}, f32[2,16,256]{2,1,0:T(8,128)S(1)}, u32[]{:S(2)}, u32[]{:S(2)}) %collective-permute-start.12) | collective-permute-done | bytes 32800 | tf_op jit(solution)/shard_map/ppermute | solution.py:20
  292.5 6.0 %collective-permute-done.13 = f32[2,16,256]{2,1,0:T(8,128)S(1)} collective-permute-done((f32[2,16,256]{2,1,0:T(8,128)S(1)}, f32[2,16,256]{2,1,0:T(8,128)S(1)}, u32[]{:S(2)}, u32[]{:S(2)}) %collective-permute-start.13) | collective-permute-done | bytes 32800 | tf_op jit(solution)/shard_map/ppermute | solution.py:20
  298.6 6.0 %collective-permute-done.14 = f32[2,16,256]{2,1,0:T(8,128)S(1)} collective-permute-done((f32[2,16,256]{2,1,0:T(8,128)S(1)}, f32[2,16,256]{2,1,0:T(8,128)S(1)}, u32[]{:S(2)}, u32[]{:S(2)}) %collective-permute-start.14) | collective-permute-done | bytes 32800 | tf_op jit(solution)/shard_map/ppermute | solution.py:20
  304.6 6.0 %collective-permute-done.15 = f32[2,16,256]{2,1,0:T(8,128)S(1)} collective-permute-done((f32[2,16,256]{2,1,0:T(8,128)S(1)}, f32[2,16,256]{2,1,0:T(8,128)S(1)}, u32[]{:S(2)}, u32[]{:S(2)}) %collective-permute-start.15) | collective-permute-done | bytes 32800 | tf_op jit(solution)/shard_map/ppermute | solution.py:20
  310.6 6.0 %collective-permute-done.16 = f32[2,16,256]{2,1,0:T(8,128)S(1)} collective-permute-done((f32[2,16,256]{2,1,0:T(8,128)S(1)}, f32[2,16,256]{2,1,0:T(8,128)S(1)}, u32[]{:S(2)}, u32[]{:S(2)}) %collective-permute-start.16) | collective-permute-done | bytes 32800 | tf_op jit(solution)/shard_map/ppermute | solution.py:20
  316.7 6.0 %collective-permute-done.17 = f32[2,16,256]{2,1,0:T(8,128)S(1)} collective-permute-done((f32[2,16,256]{2,1,0:T(8,128)S(1)}, f32[2,16,256]{2,1,0:T(8,128)S(1)}, u32[]{:S(2)}, u32[]{:S(2)}) %collective-permute-start.17) | collective-permute-done | bytes 32800 | tf_op jit(solution)/shard_map/ppermute | solution.py:20
  322.7 6.0 %collective-permute-done.18 = f32[2,16,256]{2,1,0:T(8,128)S(1)} collective-permute-done((f32[2,16,256]{2,1,0:T(8,128)S(1)}, f32[2,16,256]{2,1,0:T(8,128)S(1)}, u32[]{:S(2)}, u32[]{:S(2)}) %collective-permute-start.18) | collective-permute-done | bytes 32800 | tf_op jit(solution)/shard_map/ppermute | solution.py:20
  328.7 6.0 %collective-permute-done.19 = f32[2,16,256]{2,1,0:T(8,128)S(1)} collective-permute-done((f32[2,16,256]{2,1,0:T(8,128)S(1)}, f32[2,16,256]{2,1,0:T(8,128)S(1)}, u32[]{:S(2)}, u32[]{:S(2)}) %collective-permute-start.19) | collective-permute-done | bytes 32800 | tf_op jit(solution)/shard_map/ppermute | solution.py:20
  334.8 6.0 %collective-permute-done.20 = f32[2,16,256]{2,1,0:T(8,128)S(1)} collective-permute-done((f32[2,16,256]{2,1,0:T(8,128)S(1)}, f32[2,16,256]{2,1,0:T(8,128)S(1)}, u32[]{:S(2)}, u32[]{:S(2)}) %collective-permute-start.20) | collective-permute-done | bytes 32800 | tf_op jit(solution)/shard_map/ppermute | solution.py:20
  340.8 6.0 %collective-permute-done.21 = f32[2,16,256]{2,1,0:T(8,128)S(1)} collective-permute-done((f32[2,16,256]{2,1,0:T(8,128)S(1)}, f32[2,16,256]{2,1,0:T(8,128)S(1)}, u32[]{:S(2)}, u32[]{:S(2)}) %collective-permute-start.21) | collective-permute-done | bytes 32800 | tf_op jit(solution)/shard_map/ppermute | solution.py:20
  350.7 6.3 %collective-permute-start.5 = (f32[2,1280,128]{2,1,0:T(8,128)S(1)}, f32[2,1280,128]{2,1,0:T(8,128)S(1)}, u32[]{:S(2)}, u32[]{:S(2)}) collective-permute-start(f32[2,1280,128]{2,1,0:T(8,128)S(1)} %get-tuple-element.342), channel_id=1, source_target_pairs={{1,0},{2,1},{3,2},{4,3},{5,4},{6,5},{7,6},{8,7},{9,8},{10,9},{11,1... | collective-permute-start | bytes 3932168 | tf_op jit(solution)/shard_map/ppermute | solution.py:39
  357.0 9.2 %collective-permute-done.22 = f32[2,16,256]{2,1,0:T(8,128)S(1)} collective-permute-done((f32[2,16,256]{2,1,0:T(8,128)S(1)}, f32[2,16,256]{2,1,0:T(8,128)S(1)}, u32[]{:S(2)}, u32[]{:S(2)}) %collective-permute-start.22) | collective-permute-done | bytes 32800 | tf_op jit(solution)/shard_map/ppermute | solution.py:20
  366.6 13.7 %collective-permute-done.4 = f32[2,1280,128]{2,1,0:T(8,128)S(1)} collective-permute-done((f32[2,1280,128]{2,1,0:T(8,128)S(1)}, f32[2,1280,128]{2,1,0:T(8,128)S(1)}, u32[]{:S(2)}, u32[]{:S(2)}) %collective-permute-start.4) | collective-permute-done | bytes 1310752 | tf_op jit(solution)/shard_map/ppermute | solution.py:38
  386.9 5.4 %collective-permute-done.7 = f32[2,128,128]{2,1,0:T(8,128)S(1)} collective-permute-done((f32[2,128,128]{2,1,0:T(8,128)S(1)}, f32[2,128,128]{2,1,0:T(8,128)S(1)}, u32[]{:S(2)}, u32[]{:S(2)}) %collective-permute-start.7) | collective-permute-done | bytes 131104 | tf_op jit(solution)/shard_map/ppermute | solution.py:39
  (132 shorter events, 87.3 us)
Async XLA Ops:
  7.2 255.2 %reduce-scatter.2.cloned.1.call-start = ((), (), s32[]{:S(2)}) async-start(), calls=%async_computation.1 | async-start | bytes 557056 | tf_op jit(solution)/shard_map/reduce_scatter | solution.py:149
  8.3 6.2 %collective-permute-start = (f32[2,128,128]{2,1,0:T(8,128)S(1)}, f32[2,128,128]{2,1,0:T(8,128)S(1)}, u32[]{:S(2)}, u32[]{:S(2)}) collective-permute-start(f32[2,128,128]{2,1,0:T(8,128)S(1)} %get-tuple-element.348), channel_id=1, source_target_pairs={{0,16},{1,17},{2,18},{3,19},{4,20},{5,21},{6,22},{7,23},{8,24},{9,... | collective-permute-start | bytes 393224 | tf_op jit(solution)/shard_map/ppermute | solution.py:38
  11.7 6.9 %collective-permute-start.1 = (f32[2,128,128]{2,1,0:T(8,128)S(1)}, f32[2,128,128]{2,1,0:T(8,128)S(1)}, u32[]{:S(2)}, u32[]{:S(2)}) collective-permute-start(f32[2,128,128]{2,1,0:T(8,128)S(1)} %get-tuple-element.347), channel_id=1, source_target_pairs={{16,0},{17,1},{18,2},{19,3},{20,4},{21,5},{22,6},{23,7},{24,8},{25... | collective-permute-start | bytes 393224 | tf_op jit(solution)/shard_map/ppermute | solution.py:39
  18.6 33.0 %collective-permute-start.2 = (f32[2,1280,128]{2,1,0:T(8,128)S(1)}, f32[2,1280,128]{2,1,0:T(8,128)S(1)}, u32[]{:S(2)}, u32[]{:S(2)}) collective-permute-start(f32[2,1280,128]{2,1,0:T(8,128)S(1)} %constant_dynamic-update-slice_fusion), channel_id=1, source_target_pairs={{0,1},{1,2},{2,3},{3,4},{4,5},{5,6},{6,7},{7,8},{8,9},{9,10},{10,1... | collective-permute-start | bytes 3932168 | tf_op jit(solution)/shard_map/ppermute | solution.py:38
  20.5 31.0 %collective-permute-start.3 = (f32[2,1280,128]{2,1,0:T(8,128)S(1)}, f32[2,1280,128]{2,1,0:T(8,128)}, u32[]{:S(2)}, u32[]{:S(2)}) collective-permute-start(f32[2,1280,128]{2,1,0:T(8,128)S(1)} %constant_dynamic-update-slice_fusion), channel_id=1, source_target_pairs={{1,0},{2,1},{3,2},{4,3},{5,4},{6,5},{7,6},{8,7},{9,8},{10,9},{11,1... | collective-permute-start | bytes 3932168 | tf_op jit(solution)/shard_map/ppermute | solution.py:39
  271.3 3.4 collective-permute-start.8
  274.7 3.3 collective-permute-start.9
  278.0 3.3 collective-permute-start.10
  281.4 5.1 %collective-permute-start.11 = (f32[2,16,256]{2,1,0:T(8,128)S(1)}, f32[2,16,256]{2,1,0:T(8,128)S(1)}, u32[]{:S(2)}, u32[]{:S(2)}) collective-permute-start(f32[2,16,256]{2,1,0:T(8,128)S(1)} %collective-permute-done.10), channel_id=1, source_target_pairs={{0,1},{1,2},{2,3},{3,4},{4,5},{5,6},{6,7},{7,8},{8,9},{9,10},{10,1... | collective-permute-start | bytes 98312 | tf_op jit(solution)/shard_map/ppermute | solution.py:20
  286.5 6.0 %collective-permute-start.12 = (f32[2,16,256]{2,1,0:T(8,128)S(1)}, f32[2,16,256]{2,1,0:T(8,128)S(1)}, u32[]{:S(2)}, u32[]{:S(2)}) collective-permute-start(f32[2,16,256]{2,1,0:T(8,128)S(1)} %collective-permute-done.11), channel_id=1, source_target_pairs={{0,1},{1,2},{2,3},{3,4},{4,5},{5,6},{6,7},{7,8},{8,9},{9,10},{10,1... | collective-permute-start | bytes 98312 | tf_op jit(solution)/shard_map/ppermute | solution.py:20
  292.5 6.0 %collective-permute-start.13 = (f32[2,16,256]{2,1,0:T(8,128)S(1)}, f32[2,16,256]{2,1,0:T(8,128)S(1)}, u32[]{:S(2)}, u32[]{:S(2)}) collective-permute-start(f32[2,16,256]{2,1,0:T(8,128)S(1)} %collective-permute-done.12), channel_id=1, source_target_pairs={{0,1},{1,2},{2,3},{3,4},{4,5},{5,6},{6,7},{7,8},{8,9},{9,10},{10,1... | collective-permute-start | bytes 98312 | tf_op jit(solution)/shard_map/ppermute | solution.py:20
  298.6 6.0 %collective-permute-start.14 = (f32[2,16,256]{2,1,0:T(8,128)S(1)}, f32[2,16,256]{2,1,0:T(8,128)S(1)}, u32[]{:S(2)}, u32[]{:S(2)}) collective-permute-start(f32[2,16,256]{2,1,0:T(8,128)S(1)} %collective-permute-done.13), channel_id=1, source_target_pairs={{0,1},{1,2},{2,3},{3,4},{4,5},{5,6},{6,7},{7,8},{8,9},{9,10},{10,1... | collective-permute-start | bytes 98312 | tf_op jit(solution)/shard_map/ppermute | solution.py:20
  304.6 6.0 %collective-permute-start.15 = (f32[2,16,256]{2,1,0:T(8,128)S(1)}, f32[2,16,256]{2,1,0:T(8,128)S(1)}, u32[]{:S(2)}, u32[]{:S(2)}) collective-permute-start(f32[2,16,256]{2,1,0:T(8,128)S(1)} %collective-permute-done.14), channel_id=1, source_target_pairs={{0,1},{1,2},{2,3},{3,4},{4,5},{5,6},{6,7},{7,8},{8,9},{9,10},{10,1... | collective-permute-start | bytes 98312 | tf_op jit(solution)/shard_map/ppermute | solution.py:20
  310.6 6.0 %collective-permute-start.16 = (f32[2,16,256]{2,1,0:T(8,128)S(1)}, f32[2,16,256]{2,1,0:T(8,128)S(1)}, u32[]{:S(2)}, u32[]{:S(2)}) collective-permute-start(f32[2,16,256]{2,1,0:T(8,128)S(1)} %collective-permute-done.15), channel_id=1, source_target_pairs={{0,1},{1,2},{2,3},{3,4},{4,5},{5,6},{6,7},{7,8},{8,9},{9,10},{10,1... | collective-permute-start | bytes 98312 | tf_op jit(solution)/shard_map/ppermute | solution.py:20
  316.7 6.0 %collective-permute-start.17 = (f32[2,16,256]{2,1,0:T(8,128)S(1)}, f32[2,16,256]{2,1,0:T(8,128)S(1)}, u32[]{:S(2)}, u32[]{:S(2)}) collective-permute-start(f32[2,16,256]{2,1,0:T(8,128)S(1)} %collective-permute-done.16), channel_id=1, source_target_pairs={{0,1},{1,2},{2,3},{3,4},{4,5},{5,6},{6,7},{7,8},{8,9},{9,10},{10,1... | collective-permute-start | bytes 98312 | tf_op jit(solution)/shard_map/ppermute | solution.py:20
  322.7 6.0 %collective-permute-start.18 = (f32[2,16,256]{2,1,0:T(8,128)S(1)}, f32[2,16,256]{2,1,0:T(8,128)S(1)}, u32[]{:S(2)}, u32[]{:S(2)}) collective-permute-start(f32[2,16,256]{2,1,0:T(8,128)S(1)} %collective-permute-done.17), channel_id=1, source_target_pairs={{0,1},{1,2},{2,3},{3,4},{4,5},{5,6},{6,7},{7,8},{8,9},{9,10},{10,1... | collective-permute-start | bytes 98312 | tf_op jit(solution)/shard_map/ppermute | solution.py:20
  328.7 6.0 %collective-permute-start.19 = (f32[2,16,256]{2,1,0:T(8,128)S(1)}, f32[2,16,256]{2,1,0:T(8,128)S(1)}, u32[]{:S(2)}, u32[]{:S(2)}) collective-permute-start(f32[2,16,256]{2,1,0:T(8,128)S(1)} %collective-permute-done.18), channel_id=1, source_target_pairs={{0,1},{1,2},{2,3},{3,4},{4,5},{5,6},{6,7},{7,8},{8,9},{9,10},{10,1... | collective-permute-start | bytes 98312 | tf_op jit(solution)/shard_map/ppermute | solution.py:20
  334.8 6.0 %collective-permute-start.20 = (f32[2,16,256]{2,1,0:T(8,128)S(1)}, f32[2,16,256]{2,1,0:T(8,128)S(1)}, u32[]{:S(2)}, u32[]{:S(2)}) collective-permute-start(f32[2,16,256]{2,1,0:T(8,128)S(1)} %collective-permute-done.19), channel_id=1, source_target_pairs={{0,1},{1,2},{2,3},{3,4},{4,5},{5,6},{6,7},{7,8},{8,9},{9,10},{10,1... | collective-permute-start | bytes 98312 | tf_op jit(solution)/shard_map/ppermute | solution.py:20
  340.8 6.0 %collective-permute-start.21 = (f32[2,16,256]{2,1,0:T(8,128)S(1)}, f32[2,16,256]{2,1,0:T(8,128)S(1)}, u32[]{:S(2)}, u32[]{:S(2)}) collective-permute-start(f32[2,16,256]{2,1,0:T(8,128)S(1)} %collective-permute-done.20), channel_id=1, source_target_pairs={{0,1},{1,2},{2,3},{3,4},{4,5},{5,6},{6,7},{7,8},{8,9},{9,10},{10,1... | collective-permute-start | bytes 98312 | tf_op jit(solution)/shard_map/ppermute | solution.py:20
  346.9 19.4 %collective-permute-start.22 = (f32[2,16,256]{2,1,0:T(8,128)S(1)}, f32[2,16,256]{2,1,0:T(8,128)S(1)}, u32[]{:S(2)}, u32[]{:S(2)}) collective-permute-start(f32[2,16,256]{2,1,0:T(8,128)S(1)} %collective-permute-done.21), channel_id=1, source_target_pairs={{0,1},{1,2},{2,3},{3,4},{4,5},{5,6},{6,7},{7,8},{8,9},{9,10},{10,1... | collective-permute-start | bytes 98312 | tf_op jit(solution)/shard_map/ppermute | solution.py:20
  348.8 31.5 %collective-permute-start.4 = (f32[2,1280,128]{2,1,0:T(8,128)S(1)}, f32[2,1280,128]{2,1,0:T(8,128)S(1)}, u32[]{:S(2)}, u32[]{:S(2)}) collective-permute-start(f32[2,1280,128]{2,1,0:T(8,128)S(1)} %get-tuple-element.341), channel_id=1, source_target_pairs={{0,1},{1,2},{2,3},{3,4},{4,5},{5,6},{6,7},{7,8},{8,9},{9,10},{10,1... | collective-permute-start | bytes 3932168 | tf_op jit(solution)/shard_map/ppermute | solution.py:38
  350.7 29.6 %collective-permute-start.5 = (f32[2,1280,128]{2,1,0:T(8,128)S(1)}, f32[2,1280,128]{2,1,0:T(8,128)S(1)}, u32[]{:S(2)}, u32[]{:S(2)}) collective-permute-start(f32[2,1280,128]{2,1,0:T(8,128)S(1)} %get-tuple-element.342), channel_id=1, source_target_pairs={{1,0},{2,1},{3,2},{4,3},{5,4},{6,5},{7,6},{8,7},{9,8},{10,9},{11,1... | collective-permute-start | bytes 3932168 | tf_op jit(solution)/shard_map/ppermute | solution.py:39
  381.9 5.0 %collective-permute-start.6 = (f32[2,128,128]{2,1,0:T(8,128)S(1)}, f32[2,128,128]{2,1,0:T(8,128)S(1)}, u32[]{:S(2)}, u32[]{:S(2)}) collective-permute-start(f32[2,128,128]{2,1,0:T(8,128)S(1)} %get-tuple-element.346), channel_id=1, source_target_pairs={{0,16},{1,17},{2,18},{3,19},{4,20},{5,21},{6,22},{7,23},{8,24},{9,... | collective-permute-start | bytes 393224 | tf_op jit(solution)/shard_map/ppermute | solution.py:38
  385.3 7.0 %collective-permute-start.7 = (f32[2,128,128]{2,1,0:T(8,128)S(1)}, f32[2,128,128]{2,1,0:T(8,128)S(1)}, u32[]{:S(2)}, u32[]{:S(2)}) collective-permute-start(f32[2,128,128]{2,1,0:T(8,128)S(1)} %get-tuple-element.345), channel_id=1, source_target_pairs={{16,0},{17,1},{18,2},{19,3},{20,4},{21,5},{22,6},{23,7},{24,8},{25... | collective-permute-start | bytes 393224 | tf_op jit(solution)/shard_map/ppermute | solution.py:39
  (6 other events, 69.9 us)
Sparse Core Ops, SparseCore 0:
  117.5 144.8 reduce-scatter.1
